TPU v7x, 512 devices: a whole 4x8x8 slice. The times are simulated.
512 devices in a mesh: dp: 64 (over y, x, core), mp: 8 (over z).
Axes of the slice: x: 4, y: 8, z: 8, core: 2. Of those that a mesh axis runs over, the one named last changes fastest.
Arguments:
- tokens: bfloat16 [32768, 2048], P('dp'), may hold values from -6 to 6
- q_weight: bfloat16 [2048, 256], P('dp', 'mp'), may hold values from -0.125 to 0.125
- k_weight: bfloat16 [2048, 256], P('dp', 'mp'), may hold values from -0.125 to 0.125
- v_weight: bfloat16 [2048, 2048], P('dp', 'mp'), may hold values from -0.125 to 0.125
- adapter_down: bfloat16 [2048, 256], P(None, 'mp'), may hold values from -0.125 to 0.125
- adapter_up: bfloat16 [256, 2048], P(None, 'mp'), may hold values from -1.5 to 1.5
- lengths: int32 [4], replicated, may hold values from 1 to 16384, 32768 in all
- adapter_ids: int32 [4], replicated, may hold values from 0 to 15
- head_gain: float32 [2048], P('mp'), may hold values from 0.1 to 1.9
- out_weight: bfloat16 [2048, 2048], P('mp', 'dp'), may hold values from -0.125 to 0.125
Outputs:
- layer_out: bfloat16 [32768, 2048], P('dp', 'mp')
Inputs may be any that keep to these rules, and one draw needn't show every extreme that they name: The lengths sum to 32768 and the longest request has exactly 32768 // 2 tokens.
All inputs are finite; a program needn't handle non-finite values.
Results may differ from a plain program's by a relative error of at most 0.022.
Values may be sent and summed in bfloat16 or wider, within the bound.
A program may use at most 128 MiB of HBM per device.

v0:
```python
import math
import jax
import jax.numpy as jnp
from jax import lax
from jax.sharding import PartitionSpec as P

F = 16
R = 16
EPSILON = 1e-05


def taylor(inputs):
    squares = (inputs[..., :, None] * inputs[..., None, :]).reshape(
        inputs.shape[:-1] + (inputs.shape[-1] * inputs.shape[-1],)
    )
    constant = jnp.ones(inputs.shape[:-1] + (1,), jnp.float32)
    return jnp.concatenate([constant, 0.5 * inputs, squares * (0.25 / math.sqrt(2.0))], axis=-1)


def request_of(bounds, positions):
    return jnp.sum((positions[:, None] >= bounds[None, :]).astype(jnp.int32), axis=1)


def token_tables(lengths, adapter_ids, positions):
    bounds = jnp.cumsum(lengths)
    request = request_of(bounds, positions)
    openings = bounds - lengths
    starts = jnp.any(positions[:, None] == openings[None, :], axis=1)
    picked = request[:, None] == jnp.arange(lengths.shape[0], dtype=jnp.int32)[None, :]
    adapter = jnp.sum(jnp.where(picked, adapter_ids[None, :], 0), axis=1)
    return (request, starts, adapter)


def block_local(query, key_rows, values, request, starts):
    scores = jnp.einsum("ihd,jhd->hij", query, key_rows, preferred_element_type=jnp.float32) * 0.25
    weights = 1.0 + scores + 0.5 * scores * scores
    indexes = jnp.arange(request.shape[0], dtype=jnp.int32)
    allowed = (indexes[None, :] <= indexes[:, None]) & (request[None, :] == request[:, None])
    weights = jnp.where(allowed[None], weights, 0.0).astype(jnp.bfloat16)
    within = jnp.einsum("hij,jhe->ihe", weights, values, preferred_element_type=jnp.float32)
    query_map = taylor(query.astype(jnp.float32)).astype(jnp.bfloat16)
    key_map = taylor(key_rows.astype(jnp.float32)).astype(jnp.bfloat16)
    tail_mask = (request == request[-1]).astype(jnp.bfloat16)
    masked_keys = key_map * tail_mask[:, None, None]
    summary = jnp.einsum("ihf,ihe->hfe", masked_keys, values, preferred_element_type=jnp.float32)
    return (within, query_map, summary)


def finish(within, query_map, carried, request, starts, gains):
    follows = ((request == request[0]) & jnp.logical_not(starts[0])).astype(jnp.float32)
    cross = jnp.einsum(
        "ihf,hfe->ihe", query_map, carried.astype(jnp.bfloat16), preferred_element_type=jnp.float32
    )
    combined = within + follows[:, None, None] * cross
    factor = lax.rsqrt(jnp.mean(combined * combined, axis=-1, keepdims=True) + EPSILON)
    return (combined * factor * gains[None]).astype(jnp.bfloat16)


def carry_weights(lengths, row_count, place, blocks):
    bounds = jnp.cumsum(lengths)
    firsts = jnp.arange(blocks, dtype=jnp.int32) * row_count
    tails = request_of(bounds, firsts + (row_count - 1))
    head = request_of(bounds, place[None] * row_count)[0]
    chosen = (jnp.arange(blocks, dtype=jnp.int32) < place) & (tails == head)
    return chosen.astype(jnp.bfloat16)


def per_device(
    tokens,
    q_weight,
    k_weight,
    v_weight,
    adapter_down,
    adapter_up,
    lengths,
    adapter_ids,
    head_gain,
    out_weight,
):
    row_count = tokens.shape[0]
    qf = q_weight.shape[1]
    heads_here = qf // F
    vw = v_weight.shape[1]
    value_width = vw // heads_here
    blocks = lax.axis_size("dp")
    place = lax.axis_index("dp")
    positions = place * row_count + jnp.arange(row_count, dtype=jnp.int32)
    request, starts, adapter = token_tables(lengths, adapter_ids, positions)
    local = jnp.concatenate([q_weight, k_weight, v_weight, out_weight.T], axis=1)
    gathered = lax.all_gather(local, "dp", axis=0, tiled=True)
    q_full = gathered[:, :qf]
    k_full = gathered[:, qf : 2 * qf]
    v_full = gathered[:, 2 * qf : 2 * qf + vw]
    out_t = gathered[:, 2 * qf + vw :]
    part_low = jnp.dot(tokens, adapter_down, preferred_element_type=jnp.float32)
    owners = (
        lax.axis_index("mp") * (adapter_down.shape[1] // R)
        + jnp.arange(adapter_down.shape[1], dtype=jnp.int32) // R
    )
    part_low = jnp.where(adapter[:, None] == owners[None, :], part_low, 0.0).astype(jnp.bfloat16)
    low_rank = lax.all_gather(part_low, "mp", axis=1, tiled=True)
    query_sum = jnp.dot(tokens, q_full, preferred_element_type=jnp.float32)
    key_sum = jnp.dot(tokens, k_full, preferred_element_type=jnp.float32)
    value_sum = jnp.dot(tokens, v_full, preferred_element_type=jnp.float32)
    query = query_sum.astype(jnp.bfloat16).reshape(row_count, heads_here, F)
    key_rows = key_sum.astype(jnp.bfloat16).reshape(row_count, heads_here, F)
    values = value_sum + jnp.dot(low_rank, adapter_up, preferred_element_type=jnp.float32)
    values = values.astype(jnp.bfloat16).reshape(row_count, heads_here, value_width)
    within, query_map, summary = block_local(query, key_rows, values, request, starts)
    every = lax.all_gather(summary.astype(jnp.bfloat16), "dp")
    chosen = carry_weights(lengths, row_count, place, blocks)
    carried = jnp.dot(
        chosen[None, :], every.reshape(blocks, -1), preferred_element_type=jnp.float32
    ).reshape(summary.shape)
    gains = head_gain.reshape(heads_here, value_width)
    normed = finish(within, query_map, carried, request, starts, gains).reshape(
        row_count, heads_here * value_width
    )
    partial_terms = lax.dot_general(
        normed, out_t, (((1,), (1,)), ((), ())), preferred_element_type=jnp.float32
    )
    return lax.psum_scatter(
        partial_terms.astype(jnp.bfloat16), "mp", scatter_dimension=1, tiled=True
    )


def solution(mesh):
    placed = (
        P("dp", None),
        P("dp", "mp"),
        P("dp", "mp"),
        P("dp", "mp"),
        P(None, "mp"),
        P(None, "mp"),
        P(),
        P(),
        P("mp"),
        P("mp", "dp"),
    )
    return jax.shard_map(
        per_device, mesh=mesh, in_specs=placed, out_specs=P("dp", "mp"), check_vma=False
    )
```

profile of v0, /device:TPU:2, one launch (start us, length us, event | category | flops | bytes accessed | tf_op | source)
XLA Modules:
  0.0 274.3 jit_solution(4233398418461733872)
XLA Ops:
  6.5 1.6 pad_maximum_fusion
  8.2 0.8 reduce-window.4
  9.1 0.7 bitcast_subtract_fusion
  10.0 0.7 fusion.43
  10.6 0.7 select_reduce_fusion
  11.4 1.6 fusion.7
  13.0 31.1 %all_gather.13 = bf16[512,256]{0,1:T(8,128)(2,1)S(1)} all-gather(bf16[512,32]{0,1:T(8,128)(2,1)S(1)} %fusion.7), channel_id=1, replica_groups=mesh['dp'=64,'mp'=8] {'mp'}, dimensions={1}, use_global_device_ids=true | all-gather | bytes 294912 | tf_op jit(solution)/shard_map/all_gather | solution.py:101
  44.2 1.3 compare_convert_fusion
  45.4 0.3 fusion.44
  45.7 51.4 %all-gather.4.cloned.1.call-done = bf16[2048,576]{1,0:T(8,128)(2,1)} async-done(((bf16[32,576]{1,0:T(8,128)(2,1)}), bf16[2048,576]{1,0:T(8,128)(2,1)}) %all-gather.4.cloned.1.call-update) | async-done | bytes 2359312 | tf_op jit(solution)/shard_map/all_gather | solution.py:90
  97.1 2.1 convolution_convert_fusion.2
  99.4 2.5 fusion.6
  101.9 1.1 convolution_convert_fusion.1
  103.1 0.6 fusion.33
  103.9 0.2 fusion.14
  104.1 1.8 convolution_convert_fusion.3
  106.0 1.8 fusion.2
  107.8 82.7 %all-gather.6.cloned.1.call-done = bf16[128,273,128]{2,1,0:T(8,128)(2,1)} async-done(((bf16[2,273,128]{2,1,0:T(8,128)(2,1)}), bf16[128,273,128]{2,1,0:T(8,128)(2,1)}) %all-gather.6.cloned.1.call-update) | async-done | bytes 8945680 | tf_op jit(solution)/shard_map/all_gather | solution.py:110
  190.5 10.9 %reshape.177 = bf16[64,69888]{1,0:T(8,128)(2,1)} reshape(bf16[128,273,128]{2,1,0:T(8,128)(2,1)} %all-gather.6.cloned.1.call-done) | data formatting | bytes 17891328 | tf_op jit(solution)/shard_map/reshape | solution.py:113
  201.4 11.1 %dot_general.49 = bf16[2,273,128,64]{2,1,0,3:T(8,128)(2,1)} reshape(bf16[69888,64]{0,1:T(8,128)(2,1)} %bitcast.53) | data formatting | bytes 17891328 | tf_op jit(solution)/shard_map/dot_general | solution.py:112
  212.5 5.8 %fusion = bf16[1,2,273,128]{3,0,2,1:T(2,128)(2,1)S(1)} fusion(bf16[2,273,128,64]{2,1,0,3:T(8,128)(2,1)} %dot_general.49, s32[64]{0:T(128)S(1)} %convert_reduce_fusion.1, s32[]{:T(128)} %fusion.33, s32[]{:T(128)S(6)} %axis_index.23), kind=kOutput, calls=%fused_computation | convolution fusion | flops 8945856 | bytes 9085704 | tf_op jit(solution)/shard_map/dot_general | solution.py:112
  218.3 0.5 multiply_reduce_fusion
  219.1 3.9 %convolution_convert_fusion = bf16[512,2048]{1,0:T(8,128)(2,1)} fusion(bf16[512,256]{0,1:T(8,128)(2,1)S(1)} %bitcast.54, bf16[2048,576]{1,0:T(8,128)(2,1)} %all-gather.4.cloned.1.call-done), kind=kOutput, calls=%fused_computation.2 | convolution fusion | flops 537919488 | bytes 3407872 | tf_op jit(solution)/shard_map/dot_general | solution.py:119
  223.0 44.7 %reduce-scatter.2.cloned.1.call-done = bf16[512,256]{1,0:T(8,128)(2,1)} async-done(((bf16[512,2048]{1,0:T(8,128)(2,1)}), bf16[512,256]{1,0:T(8,128)(2,1)}) %reduce-scatter.2.cloned.1.call-update) | async-done | bytes 262160 | tf_op jit(solution)/shard_map/reduce_scatter | solution.py:122
  (29 shorter events, 1.0 us)
Async XLA Ops:
  6.5 4.8 %copy-start = (bf16[512,2048]{1,0:T(8,128)(2,1)S(1)}, bf16[512,2048]{1,0:T(8,128)(2,1)}, u32[]{:S(2)}) copy-start(bf16[512,2048]{1,0:T(8,128)(2,1)} %param.10) | copy-start | bytes 6291460
  6.5 38.9 %copy-start.1 = (bf16[256,256]{1,0:T(8,128)(2,1)S(1)}, bf16[256,256]{1,0:T(8,128)(2,1)}, u32[]{:S(2)}) copy-start(bf16[256,256]{1,0:T(8,128)(2,1)} %param.15) | copy-start | bytes 393220
  6.5 90.6 %all-gather.4.cloned.1.call-start = ((), (), s32[]{:S(2)}) async-start(), calls=%async_computation.1 | async-start | bytes 2662400 | tf_op jit(solution)/shard_map/all_gather | solution.py:90
  8.2 182.3 %all-gather.6.cloned.1.call-start = ((), (), s32[]{:S(2)}) async-start(), calls=%async_computation.3 | async-start | bytes 9318400 | tf_op jit(solution)/shard_map/all_gather | solution.py:110
  103.1 164.7 %reduce-scatter.2.cloned.1.call-start = ((), (), s32[]{:S(2)}) async-start(), calls=%async_computation.2 | async-start | bytes 2359296 | tf_op jit(solution)/shard_map/reduce_scatter | solution.py:122
  212.5 5.8 %copy-start.3 = (f32[2,128,512]{2,1,0:T(8,128)S(1)}, f32[2,128,512]{2,1,0:T(8,128)}, u32[]{:S(2)}) copy-start(f32[2,128,512]{2,1,0:T(8,128)} %fusion.2) | copy-start | bytes 1572868
  218.3 0.7 copy-start.2
Sparse Core Ops, SparseCore 0:
  10.7 86.4 all-gather.3
  103.2 87.2 all-gather.5
  223.1 44.5 reduce-scatter.1
where the time goes:
time: 275 us; the launch traced here: 274 us
  waiting for transfers between devices  179 us (65%)
  blocking collectives  31.1 us (11%)
  local copies, waits for them, and re-layouts  22.8 us (8%)
  matrix products  21.4 us (8%)
  between operations  13.3 us (5%)
  other arithmetic  6.59 us (2%)
    all_gather x1, waiting for transfers between devices, per_device(): every = lax.all_gather(summary.astype(jnp.bfloat16), 'dp')  82.7 us
    all_gather x1, waiting for transfers between devices, per_device(): gathered = lax.all_gather(local, 'dp', axis=0, tiled=True)  51.4 us
    reduce_scatter x1, waiting for transfers between devices, per_device(): lax.psum_scatter(partial_terms.astype(jnp.bfloat16), 'mp', scatter_dimens...  44.7 us
    all_gather x1, blocking collectives, per_device(): low_rank = lax.all_gather(part_low, 'mp', axis=1, tiled=True)  31.1 us
    dot_general x1, local copies, waits for them, and re-layouts, per_device(): jnp.dot(chosen[None, :], every.reshape(blocks, -1), preferred_element_typ...  11.1 us
    reshape x1, local copies, waits for them, and re-layouts, per_device(): every.reshape(blocks, -1)  10.9 us
    dot_general x1, matrix products, per_device(): jnp.dot(chosen[None, :], every.reshape(blocks, -1), preferred_element_typ...  5.76 us
  transfers between devices with their start and end apart: 3, of which 3 were waited for; matrix products, arithmetic and copies ran while one was open for 4% of the time, Pallas kernels for 0%

commit v1 on v0

--- a/solution.py
+++ b/solution.py
@@ -98,7 +98,13 @@
         + jnp.arange(adapter_down.shape[1], dtype=jnp.int32) // R
     )
     part_low = jnp.where(adapter[:, None] == owners[None, :], part_low, 0.0).astype(jnp.bfloat16)
-    low_rank = lax.all_gather(part_low, "mp", axis=1, tiled=True)
+    low_rank = lax.all_to_all(
+        jnp.concatenate(lax.axis_size("mp") * [part_low], axis=1),
+        "mp",
+        split_axis=1,
+        concat_axis=1,
+        tiled=True,
+    )
     query_sum = jnp.dot(tokens, q_full, preferred_element_type=jnp.float32)
     key_sum = jnp.dot(tokens, k_full, preferred_element_type=jnp.float32)
     value_sum = jnp.dot(tokens, v_full, preferred_element_type=jnp.float32)

time: 275 us -> 275 us (level)
  the two profiles are of different devices: /device:TPU:2 before, /device:TPU:12 now
where the time goes in v1:
time: 275 us; the launch traced here: 274 us
  waiting for transfers between devices  195 us (71%)
  local copies, waits for them, and re-layouts  27.2 us (10%)
  matrix products  22 us (8%)
  between operations  13.3 us (5%)
  starting transfers between devices  10.4 us (4%)
  other arithmetic  5.93 us (2%)
    all_gather x1, waiting for transfers between devices, per_device(): every = lax.all_gather(summary.astype(jnp.bfloat16), 'dp')  83 us
    all_gather x1, waiting for transfers between devices, per_device(): gathered = lax.all_gather(local, 'dp', axis=0, tiled=True)  57.9 us
    reduce_scatter x1, waiting for transfers between devices, per_device(): lax.psum_scatter(partial_terms.astype(jnp.bfloat16), 'mp', scatter_dimens...  44.8 us
    dot_general x1, local copies, waits for them, and re-layouts, per_device(): jnp.dot(chosen[None, :], every.reshape(blocks, -1), preferred_element_typ...  11.1 us
    reshape x1, local copies, waits for them, and re-layouts, per_device(): every.reshape(blocks, -1)  10.9 us
    all_to_all x1, starting transfers between devices, per_device(): lax.all_to_all(jnp.concatenate(lax.axis_size('mp') * [part_low], axis=1),...  10.3 us
    all_to_all x1, waiting for transfers between devices, per_device(): lax.all_to_all(jnp.concatenate(lax.axis_size('mp') * [part_low], axis=1),...  9.76 us
    dot_general x1, matrix products, per_device(): jnp.dot(chosen[None, :], every.reshape(blocks, -1), preferred_element_typ...  5.76 us
  transfers between devices with their start and end apart: 4, of which 4 were waited for; matrix products, arithmetic and copies ran while one was open for 6% of the time, Pallas kernels for 0%

profile of v1, /device:TPU:12, one launch (start us, length us, event | category | flops | bytes accessed | tf_op | source)
XLA Modules:
  0.0 274.2 jit_solution(6763296668605365871)
XLA Ops:
  6.5 1.6 pad_maximum_fusion
  8.2 0.8 reduce-window.4
  9.1 0.7 select_reduce_fusion
  9.8 2.3 constant_dynamic-update-slice_fusion.7
  12.1 0.6 constant_dynamic-update-slice_fusion.6
  12.7 0.6 constant_dynamic-update-slice_fusion.5
  15.2 0.6 constant_dynamic-update-slice_fusion.1
  16.4 10.3 %all-to-all-start = ((bf16[512,8,32]{0,2,1:T(8,128)(2,1)}), bf16[512,8,32]{0,2,1:T(8,128)(2,1)S(1)}, u32[]{:S(2)}, u32[]{:S(2)}) async-start(bf16[512,8,32]{0,2,1:T(8,128)(2,1)} %bitcast.4), calls=%async_computation | async-start | bytes 524288 | tf_op jit(solution)/shard_map/all_to_all | solution.py:101
  27.0 0.6 fusion.43
  27.6 1.2 compare_convert_fusion
  28.9 9.8 %all-to-all-done = bf16[512,8,32]{0,2,1:T(8,128)(2,1)S(1)} async-done(((bf16[512,8,32]{0,2,1:T(8,128)(2,1)}), bf16[512,8,32]{0,2,1:T(8,128)(2,1)S(1)}, u32[]{:S(2)}, u32[]{:S(2)}) %all-to-all-start) | async-done | bytes 262176 | tf_op jit(solution)/shard_map/all_to_all | solution.py:101
  38.9 57.9 %all-gather.4.cloned.1.call-done = bf16[2048,576]{1,0:T(8,128)(2,1)} async-done(((bf16[32,576]{1,0:T(8,128)(2,1)}), bf16[2048,576]{1,0:T(8,128)(2,1)}) %all-gather.4.cloned.1.call-update) | async-done | bytes 2359312 | tf_op jit(solution)/shard_map/all_gather | solution.py:90
  96.8 2.1 convolution_convert_fusion.2
  99.0 2.5 fusion.6
  101.5 1.1 convolution_convert_fusion.1
  102.8 0.6 fusion.33
  103.7 1.8 convolution_convert_fusion.3
  105.6 1.8 fusion.2
  107.4 83.0 %all-gather.6.cloned.1.call-done = bf16[128,273,128]{2,1,0:T(8,128)(2,1)} async-done(((bf16[2,273,128]{2,1,0:T(8,128)(2,1)}), bf16[128,273,128]{2,1,0:T(8,128)(2,1)}) %all-gather.6.cloned.1.call-update) | async-done | bytes 8945680 | tf_op jit(solution)/shard_map/all_gather | solution.py:116
  190.4 10.9 %reshape.179 = bf16[64,69888]{1,0:T(8,128)(2,1)} reshape(bf16[128,273,128]{2,1,0:T(8,128)(2,1)} %all-gather.6.cloned.1.call-done) | data formatting | bytes 17891328 | tf_op jit(solution)/shard_map/reshape | solution.py:119
  201.3 11.1 %dot_general.49 = bf16[2,273,128,64]{2,1,0,3:T(8,128)(2,1)} reshape(bf16[69888,64]{0,1:T(8,128)(2,1)} %bitcast.55) | data formatting | bytes 17891328 | tf_op jit(solution)/shard_map/dot_general | solution.py:118
  212.4 5.8 %fusion = bf16[1,2,273,128]{3,0,2,1:T(2,128)(2,1)S(1)} fusion(bf16[2,273,128,64]{2,1,0,3:T(8,128)(2,1)} %dot_general.49, s32[64]{0:T(128)S(1)} %convert_reduce_fusion.1, s32[]{:T(128)} %fusion.33, s32[]{:T(128)S(6)} %axis_index.23), kind=kOutput, calls=%fused_computation | convolution fusion | flops 8945856 | bytes 9085704 | tf_op jit(solution)/shard_map/dot_general | solution.py:118
  219.0 3.9 %convolution_convert_fusion = bf16[512,2048]{1,0:T(8,128)(2,1)} fusion(bf16[512,256]{0,1:T(8,128)(2,1)S(1)} %bitcast.57, bf16[2048,576]{1,0:T(8,128)(2,1)} %all-gather.4.cloned.1.call-done), kind=kOutput, calls=%fused_computation.2 | convolution fusion | flops 537919488 | bytes 3407872 | tf_op jit(solution)/shard_map/dot_general | solution.py:125
  222.9 44.8 %reduce-scatter.2.cloned.1.call-done = bf16[512,256]{1,0:T(8,128)(2,1)} async-done(((bf16[512,2048]{1,0:T(8,128)(2,1)}), bf16[512,256]{1,0:T(8,128)(2,1)}) %reduce-scatter.2.cloned.1.call-update) | async-done | bytes 262160 | tf_op jit(solution)/shard_map/reduce_scatter | solution.py:128
  (39 shorter events, 4.4 us)
Async XLA Ops:
  6.5 3.3 %copy-start = (bf16[512,2048]{1,0:T(8,128)(2,1)S(1)}, bf16[512,2048]{1,0:T(8,128)(2,1)}, u32[]{:S(2)}) copy-start(bf16[512,2048]{1,0:T(8,128)(2,1)} %param.10) | copy-start | bytes 6291460
  6.5 20.3 %copy-start.3 = (s32[4]{0:T(128)S(1)}, s32[4]{0:T(128)}, u32[]{:S(2)}) copy-start(s32[4]{0:T(128)} %param.16) | copy-start | bytes 52
  6.5 32.1 %copy-start.1 = (bf16[256,256]{1,0:T(8,128)(2,1)S(1)}, bf16[256,256]{1,0:T(8,128)(2,1)}, u32[]{:S(2)}) copy-start(bf16[256,256]{1,0:T(8,128)(2,1)} %param.15) | copy-start | bytes 393220
  6.5 90.2 %all-gather.4.cloned.1.call-start = ((), (), s32[]{:S(2)}) async-start(), calls=%async_computation.2 | async-start | bytes 2662400 | tf_op jit(solution)/shard_map/all_gather | solution.py:90
  16.4 22.2 %all-to-all-start = ((bf16[512,8,32]{0,2,1:T(8,128)(2,1)}), bf16[512,8,32]{0,2,1:T(8,128)(2,1)S(1)}, u32[]{:S(2)}, u32[]{:S(2)}) async-start(bf16[512,8,32]{0,2,1:T(8,128)(2,1)} %bitcast.4), calls=%async_computation | async-start | bytes 524288 | tf_op jit(solution)/shard_map/all_to_all | solution.py:101
  26.7 163.7 %all-gather.6.cloned.1.call-start = ((), (), s32[]{:S(2)}) async-start(), calls=%async_computation.4 | async-start | bytes 9318400 | tf_op jit(solution)/shard_map/all_gather | solution.py:116
  102.7 165.0 %reduce-scatter.2.cloned.1.call-start = ((), (), s32[]{:S(2)}) async-start(), calls=%async_computation.3 | async-start | bytes 2359296 | tf_op jit(solution)/shard_map/reduce_scatter | solution.py:128
  212.4 5.8 %copy-start.4 = (f32[2,128,512]{2,1,0:T(8,128)S(1)}, f32[2,128,512]{2,1,0:T(8,128)}, u32[]{:S(2)}) copy-start(f32[2,128,512]{2,1,0:T(8,128)} %fusion.2) | copy-start | bytes 1572868
  218.2 0.7 copy-start.2
Sparse Core Ops, SparseCore 0:
  10.7 86.0 all-gather.3
  102.8 87.5 all-gather.5
  223.0 44.6 reduce-scatter.1
